TPU v7x, 32 devices: a whole 2x2x4 slice. The times are simulated.
32 devices in a mesh: batch: 16 (over z, y, core), tensor: 2 (over x).
Axes of the slice: x: 2, y: 2, z: 4, core: 2. Of those that a mesh axis runs over, the one named last changes fastest.
Arguments:
- block_in: bfloat16 [2, 16384, 1024], P(None, ('batch', 'tensor')), may hold values from -6 to 6
- lengths: int32 [2, 16, 4], P(None, 'batch'), may hold values from 1 to 512, 1024 in all within a row
- norm_gains: float32 [3, 1024], replicated, may hold values from 0.5 to 1.5
- qkv_weight: bfloat16 [3, 1024, 1024], P(None, 'batch', 'tensor'), may hold values from -0.1875 to 0.1875
- head_scale: float32 [16], P('tensor'), may hold values from 0.5 to 2
- out_weight: bfloat16 [1024, 1024], P('tensor', 'batch'), may hold values from -0.1875 to 0.1875
- up_weight: bfloat16 [1024, 4096], P('batch', 'tensor'), may hold values from -0.7875 to 0.7875
- mid_gain: float32 [4096], P('tensor'), may hold values from 0.5 to 1.5
- down_weight: bfloat16 [4096, 1024], P('tensor', 'batch'), may hold values from -0.39375 to 0.39375
- cotangent: bfloat16 [2, 16384, 1024], P(None, ('batch', 'tensor')), may hold values from -6 to 6
Outputs:
- block_out: bfloat16 [2, 16384, 1024], P(None, ('batch', 'tensor'))
- grad_in: bfloat16 [2, 16384, 1024], P(None, ('batch', 'tensor'))
- grad_gains: float32 [3, 1024], replicated
- grad_qkv: float32 [3, 1024, 1024], P(None, 'batch', 'tensor')
- grad_scale: float32 [16], P('tensor')
- grad_proj: float32 [1024, 1024], P('tensor', 'batch')
- grad_up: float32 [1024, 4096], P('batch', 'tensor')
- grad_mid: float32 [4096], P('tensor')
- grad_down: float32 [4096, 1024], P('tensor', 'batch')
Inputs may be any that keep to these rules, and one draw needn't show every extreme that they name: lengths[m, b] holds the lengths of the 4 sequences packed in order into the 1024 rows of group b in micro-batch m; they sum to 1024.
All inputs are finite; a program needn't handle non-finite values.
Results may differ from a plain program's by a relative error of at most 0.019.
Values may be sent and summed in bfloat16 or wider, within the bound.
No kernel may reach another device: no remote copies, remote signals or barrier semaphores. Data moves between devices by JAX's collectives and lax.ppermute only.
A program may use at most 256 MiB of HBM per device.

v0:
```python
import jax
import jax.numpy as jnp
from jax import lax
from jax.sharding import PartitionSpec as P

eps = 1e-05


def normalize(values):
    centred = values - jnp.mean(values, axis=-1, keepdims=True)
    factor = lax.rsqrt(jnp.mean(centred * centred, axis=-1, keepdims=True) + eps)
    return (centred * factor, factor)


def norm_back(unit, factor, grad):
    return factor * (
        grad
        - jnp.mean(grad, axis=-1, keepdims=True)
        - unit * jnp.mean(grad * unit, axis=-1, keepdims=True)
    )


def segment_ids(seq_lengths, group_rows):
    places = jnp.arange(group_rows, dtype=jnp.int32)
    ends = jnp.cumsum(seq_lengths)
    seg_ids = jnp.sum((places[:, None] >= ends[None, :]).astype(jnp.int32), axis=1)
    return (seg_ids, places)


def visible_block(seg_ids, places, first_row, block_rows):
    seg_block = lax.dynamic_slice_in_dim(seg_ids, first_row, block_rows, 0)
    place_block = lax.dynamic_slice_in_dim(places, first_row, block_rows, 0)
    return (seg_block[:, None] == seg_ids[None, :]) & (place_block[:, None] >= places[None, :])


def attend_forward(queries, all_keys, values, seg_ids, places, block_rows, factor):
    group_rows = queries.shape[0]

    def one_block(first_row):
        query_block = lax.dynamic_slice_in_dim(queries, first_row, block_rows, 0)
        visible = visible_block(seg_ids, places, first_row, block_rows)
        scores = (
            jnp.einsum("qhd,khd->hqk", query_block, all_keys, preferred_element_type=jnp.float32)
            * factor
        )
        scores = jnp.where(visible[None], scores, -1e30)
        row_max = jnp.max(scores, axis=-1, keepdims=True)
        shifted = jnp.exp(scores - row_max)
        row_sum = jnp.sum(shifted, axis=-1, keepdims=True)
        weights_low = (shifted / row_sum).astype(jnp.bfloat16)
        attended = jnp.einsum(
            "hqk,khd->qhd", weights_low, values, preferred_element_type=jnp.float32
        )
        return (attended, (row_max + jnp.log(row_sum))[..., 0])

    firsts = jnp.arange(group_rows // block_rows, dtype=jnp.int32) * block_rows
    attended, log_sums = lax.map(one_block, firsts)
    return (attended.reshape(queries.shape), log_sums)


def attend_backward(
    queries, all_keys, values, seg_ids, places, block_rows, factor, log_sums, out_grad
):
    group_rows = queries.shape[0]

    def one_block(totals, pieces):
        key_grad, value_grad = totals
        first_row, log_block = pieces
        query_block = lax.dynamic_slice_in_dim(queries, first_row, block_rows, 0)
        grad_block = lax.dynamic_slice_in_dim(out_grad, first_row, block_rows, 0)
        visible = visible_block(seg_ids, places, first_row, block_rows)
        scores = (
            jnp.einsum("qhd,khd->hqk", query_block, all_keys, preferred_element_type=jnp.float32)
            * factor
        )
        scores = jnp.where(visible[None], scores, -1e30)
        probs = jnp.exp(scores - log_block[..., None])
        value_grad = value_grad + jnp.einsum(
            "hqk,qhd->khd",
            probs.astype(jnp.bfloat16),
            grad_block,
            preferred_element_type=jnp.float32,
        )
        prob_grad = jnp.einsum(
            "qhd,khd->hqk", grad_block, values, preferred_element_type=jnp.float32
        )
        inner = jnp.sum(probs * prob_grad, axis=-1, keepdims=True)
        score_grad = (probs * (prob_grad - inner)).astype(jnp.bfloat16)
        query_grad = (
            jnp.einsum("hqk,khd->qhd", score_grad, all_keys, preferred_element_type=jnp.float32)
            * factor
        )
        key_grad = (
            key_grad
            + jnp.einsum(
                "hqk,qhd->khd", score_grad, query_block, preferred_element_type=jnp.float32
            )
            * factor
        )
        return ((key_grad, value_grad), query_grad)

    zero_grad = jnp.zeros(queries.shape, jnp.float32)
    firsts = jnp.arange(group_rows // block_rows, dtype=jnp.int32) * block_rows
    (key_grad, value_grad), query_grad = lax.scan(
        one_block, (zero_grad, zero_grad), (firsts, log_sums)
    )
    return (query_grad.reshape(queries.shape), key_grad, value_grad)


def body(
    block_in,
    lengths,
    norm_gains,
    qkv_weight,
    head_scale,
    out_weight,
    up_weight,
    mid_gain,
    down_weight,
    cotangent,
):
    tensor_count = lax.axis_size("tensor")
    tensor_rank = lax.axis_index("tensor")
    qkv_full, out_full, up_full, down_full = (
        lax.all_gather(qkv_weight, "batch", axis=1, tiled=True),
        lax.all_gather(out_weight, "batch", axis=1, tiled=True),
        lax.all_gather(up_weight, "batch", axis=0, tiled=True),
        lax.all_gather(down_weight, "batch", axis=1, tiled=True),
    )
    micro_count, own_rows, model_width = block_in.shape
    group_rows = own_rows * tensor_count
    local_heads = head_scale.shape[0]
    head_size = qkv_full.shape[2] // local_heads
    local_hidden = mid_gain.shape[0]
    hidden_total = local_hidden * tensor_count
    block_rows = min(512, group_rows)
    factor = head_size ** (-0.5)
    heads_shape = (group_rows, local_heads, head_size)
    row_start = tensor_rank * own_rows
    qkv_acc = jnp.zeros(qkv_full.shape, jnp.float32)
    proj_acc = jnp.zeros(out_full.shape, jnp.float32)
    up_acc = jnp.zeros(up_full.shape, jnp.float32)
    down_acc = jnp.zeros(down_full.shape, jnp.float32)
    first_gain = jnp.zeros((model_width,), jnp.float32)
    second_gain = jnp.zeros((model_width,), jnp.float32)
    third_gain = jnp.zeros((model_width,), jnp.float32)
    mid_acc = jnp.zeros((local_hidden,), jnp.float32)
    scale_acc = jnp.zeros((local_heads,), jnp.float32)
    outputs = []
    input_grads = []
    for micro_step in range(micro_count):
        seg_ids, places = segment_ids(lengths[micro_step, 0], group_rows)
        x_rows = block_in[micro_step].astype(jnp.float32)
        input_unit, input_factor = normalize(x_rows)
        first_own = (input_unit * norm_gains[0]).astype(jnp.bfloat16)
        first_all = lax.all_gather(first_own, "tensor", axis=0, tiled=True)
        projected = jnp.einsum(
            "gd,cde->cge", first_all, qkv_full, preferred_element_type=jnp.float32
        ).astype(jnp.bfloat16)
        queries = projected[0].reshape(heads_shape)
        all_keys = projected[1].reshape(heads_shape)
        values = projected[2].reshape(heads_shape)
        attended, log_sums = attend_forward(
            queries, all_keys, values, seg_ids, places, block_rows, factor
        )
        scaled = (attended * head_scale[None, :, None]).astype(jnp.bfloat16).reshape(group_rows, -1)
        whole_mixed = lax.psum(
            jnp.dot(scaled, out_full, preferred_element_type=jnp.float32), "tensor"
        )
        mixed_own = lax.dynamic_slice_in_dim(whole_mixed, row_start, own_rows, 0)
        mixed_unit, mixed_factor = normalize(mixed_own)
        resid = x_rows + mixed_unit * norm_gains[1]
        resid_unit, resid_factor = normalize(resid)
        third_own = (resid_unit * norm_gains[2]).astype(jnp.bfloat16)
        third_all = lax.all_gather(third_own, "tensor", axis=0, tiled=True)
        hidden = jnp.dot(third_all, up_full, preferred_element_type=jnp.float32)
        activated = jax.nn.gelu(hidden)
        act_sum, act_squares = lax.psum(
            (jnp.sum(activated, axis=1), jnp.sum(activated * activated, axis=1)), "tensor"
        )
        act_mean = act_sum / hidden_total
        act_factor = lax.rsqrt(act_squares / hidden_total - act_mean * act_mean + eps)[:, None]
        act_unit = (activated - act_mean[:, None]) * act_factor
        narrow = (act_unit * mid_gain).astype(jnp.bfloat16)
        feed_own = lax.psum_scatter(
            jnp.dot(narrow, down_full, preferred_element_type=jnp.float32).astype(jnp.bfloat16),
            "tensor",
            scatter_dimension=0,
            tiled=True,
        ).astype(jnp.float32)
        outputs.append((resid + feed_own).astype(jnp.bfloat16))
        out_rows = cotangent[micro_step].astype(jnp.float32)
        feed_grad = lax.all_gather(out_rows.astype(jnp.bfloat16), "tensor", axis=0, tiled=True)
        down_acc = down_acc + jnp.einsum(
            "gf,gd->fd", narrow, feed_grad, preferred_element_type=jnp.float32
        )
        narrow_grad = jnp.einsum(
            "gd,fd->gf", feed_grad, down_full, preferred_element_type=jnp.float32
        )
        mid_acc = mid_acc + jnp.sum(narrow_grad * act_unit, axis=0)
        gained = narrow_grad * mid_gain
        back_sum, back_inner = lax.psum(
            (jnp.sum(gained, axis=1), jnp.sum(gained * act_unit, axis=1)), "tensor"
        )
        act_grad = act_factor * (
            gained
            - back_sum[:, None] / hidden_total
            - act_unit * back_inner[:, None] / hidden_total
        )
        gelu_pull = jax.vjp(jax.nn.gelu, hidden)[1]
        hidden_grad = gelu_pull(act_grad)[0].astype(jnp.bfloat16)
        up_acc = up_acc + jnp.einsum(
            "gd,gf->df", third_all, hidden_grad, preferred_element_type=jnp.float32
        )
        third_grad = lax.psum_scatter(
            jnp.einsum("gf,df->gd", hidden_grad, up_full, preferred_element_type=jnp.float32),
            "tensor",
            scatter_dimension=0,
            tiled=True,
        )
        third_gain = third_gain + jnp.sum(third_grad * resid_unit, axis=0)
        resid_grad = out_rows + norm_back(resid_unit, resid_factor, third_grad * norm_gains[2])
        second_gain = second_gain + jnp.sum(resid_grad * mixed_unit, axis=0)
        mixed_grad = norm_back(mixed_unit, mixed_factor, resid_grad * norm_gains[1]).astype(
            jnp.bfloat16
        )
        mixed_all = lax.all_gather(mixed_grad, "tensor", axis=0, tiled=True)
        proj_acc = proj_acc + jnp.einsum(
            "ge,gd->ed", scaled, mixed_all, preferred_element_type=jnp.float32
        )
        scaled_grad = jnp.einsum(
            "gd,ed->ge", mixed_all, out_full, preferred_element_type=jnp.float32
        ).reshape(heads_shape)
        scale_acc = scale_acc + jnp.sum(scaled_grad * attended, axis=(0, 2))
        attended_grad = (scaled_grad * head_scale[None, :, None]).astype(jnp.bfloat16)
        query_grad, key_grad, value_grad = attend_backward(
            queries, all_keys, values, seg_ids, places, block_rows, factor, log_sums, attended_grad
        )
        proj_grads = jnp.stack(
            [
                query_grad.reshape(group_rows, -1),
                key_grad.reshape(group_rows, -1),
                value_grad.reshape(group_rows, -1),
            ]
        ).astype(jnp.bfloat16)
        qkv_acc = qkv_acc + jnp.einsum(
            "gd,cge->cde", first_all, proj_grads, preferred_element_type=jnp.float32
        )
        first_grad = lax.psum_scatter(
            jnp.einsum(
                "cge,cde->gd", proj_grads, qkv_full, preferred_element_type=jnp.float32
            ).astype(jnp.bfloat16),
            "tensor",
            scatter_dimension=0,
            tiled=True,
        ).astype(jnp.float32)
        first_gain = first_gain + jnp.sum(first_grad * input_unit, axis=0)
        input_grads.append(
            (resid_grad + norm_back(input_unit, input_factor, first_grad * norm_gains[0])).astype(
                jnp.bfloat16
            )
        )
    qkv_grad, proj_grad, up_grad, down_grad = (
        lax.psum_scatter(
            qkv_acc.astype(jnp.bfloat16), "batch", scatter_dimension=1, tiled=True
        ).astype(jnp.float32),
        lax.psum_scatter(
            proj_acc.astype(jnp.bfloat16), "batch", scatter_dimension=1, tiled=True
        ).astype(jnp.float32),
        lax.psum_scatter(
            up_acc.astype(jnp.bfloat16), "batch", scatter_dimension=0, tiled=True
        ).astype(jnp.float32),
        lax.psum_scatter(
            down_acc.astype(jnp.bfloat16), "batch", scatter_dimension=1, tiled=True
        ).astype(jnp.float32),
    )
    mid_full = lax.dynamic_update_slice_in_dim(
        jnp.zeros((hidden_total,), jnp.float32), mid_acc, tensor_rank * local_hidden, 0
    )
    scale_full = lax.dynamic_update_slice_in_dim(
        jnp.zeros((local_heads * tensor_count,), jnp.float32),
        scale_acc,
        tensor_rank * local_heads,
        0,
    )
    gains_sum, mid_sum, scale_sum = lax.psum(
        (jnp.stack([first_gain, second_gain, third_gain]), mid_full, scale_full),
        ("batch", "tensor"),
    )
    mid_own = lax.dynamic_slice_in_dim(mid_sum, tensor_rank * local_hidden, local_hidden, 0)
    scale_own = lax.dynamic_slice_in_dim(scale_sum, tensor_rank * local_heads, local_heads, 0)
    return (
        jnp.stack(outputs),
        jnp.stack(input_grads),
        gains_sum,
        qkv_grad,
        scale_own,
        proj_grad,
        up_grad,
        mid_own,
        down_grad,
    )


def solution(mesh):
    in_specs = (
        P(None, ("batch", "tensor"), None),
        P(None, "batch", None),
        P(),
        P(None, "batch", "tensor"),
        P("tensor"),
        P("tensor", "batch"),
        P("batch", "tensor"),
        P("tensor"),
        P("tensor", "batch"),
        P(None, ("batch", "tensor"), None),
    )
    out_specs = (
        P(None, ("batch", "tensor"), None),
        P(None, ("batch", "tensor"), None),
        P(),
        P(None, "batch", "tensor"),
        P("tensor"),
        P("tensor", "batch"),
        P("batch", "tensor"),
        P("tensor"),
        P("tensor", "batch"),
    )
    return jax.shard_map(body, mesh=mesh, in_specs=in_specs, out_specs=out_specs, check_vma=False)
```

profile of v0, /device:TPU:0, one launch (start us, length us, event | category | flops | bytes accessed | tf_op | source)
XLA Modules:
  0.0 1623.8 jit_solution(3066448921522963415)
XLA Ops:
  16.8 32.0 %all-gather.15.cloned.1.call-done = bf16[1024,1024]{1,0:T(8,128)(2,1)} async-done(((bf16[512,1024]{1,0:T(8,128)(2,1)}), bf16[1024,1024]{1,0:T(8,128)(2,1)}) %all-gather.15.cloned.1.call-update) | async-done | bytes 2097168 | tf_op jit(solution)/shard_map/all_gather | solution.py:156
  48.8 47.4 %all-gather.17.cloned.1.call-done = bf16[3,1024,512]{2,1,0:T(8,128)(2,1)} async-done(((bf16[3,64,512]{2,1,0:T(8,128)(2,1)}), bf16[3,1024,512]{2,1,0:T(8,128)(2,1)}) %all-gather.17.cloned.1.call-update) | async-done | bytes 3145744 | tf_op jit(solution)/shard_map/all_gather | solution.py:125
  105.5 75.3 %while.58 = (s32[]{:T(128)}, f32[2,512,8,64]{1,0,3,2:T(2,128)}, f32[2,8,512]{2,1,0:T(8,128)S(1)}, s32[2]{0:T(128)S(1)}, s32[1024]{0:T(1024)S(1)}, /*index=5*/s32...) while((s32[]{:T(128)}, f32[2,512,8,64]{1,0,3,2:T(2,128)}, ...), condition=%wide.region_7.8_spmd.clone, body=%wide.region_4.7_spmd.clone.sunk | while | flops 1125642240 | bytes 60444856 | solution.py:57
  123.5 19.6 %dynamic_update_slice.49 = f32[2,512,8,64]{1,0,3,2:T(2,128)} dynamic-update-slice(f32[2,512,8,64]{1,0,3,2:T(2,128)} %get-tuple-element.984, f32[1,512,8,64]{1,0,3,2:T(1,128)S(1)} %copy.129, s32[]{:T(128)} %get-tuple-element.983, s32[]{:T(128)} %constant.141.clone.1..sunk, s32[]{:T(128)} %constant.141.clone.1..sunk, s32[]{:T(128)} %constant.141.clone.1..sunk) | dynamic-update-slice | bytes 2097156 | tf_op jit(solution)/shard_map/while/body/jit(dynamic_update_index_in_dim)/dynamic_update_slice | solution.py:57
  160.8 19.6 %dynamic_update_slice.49 = f32[2,512,8,64]{1,0,3,2:T(2,128)} dynamic-update-slice(f32[2,512,8,64]{1,0,3,2:T(2,128)} %get-tuple-element.984, f32[1,512,8,64]{1,0,3,2:T(1,128)S(1)} %copy.129, s32[]{:T(128)} %get-tuple-element.983, s32[]{:T(128)} %constant.141.clone.1..sunk, s32[]{:T(128)} %constant.141.clone.1..sunk, s32[]{:T(128)} %constant.141.clone.1..sunk) | dynamic-update-slice | bytes 2097156 | tf_op jit(solution)/shard_map/while/body/jit(dynamic_update_index_in_dim)/dynamic_update_slice | solution.py:57
  191.5 74.9 %while.59 = (s32[]{:T(128)}, f32[2,512,8,64]{1,0,3,2:T(2,128)}, f32[2,8,512]{2,1,0:T(8,128)S(1)}, s32[2]{0:T(128)S(1)}, s32[1024]{0:T(1024)S(1)}, /*index=5*/s32...) while((s32[]{:T(128)}, f32[2,512,8,64]{1,0,3,2:T(2,128)}, ...), condition=%wide.region_25.26_spmd.clone, body=%wide.region_22.25_spmd.clone.sunk | while | flops 1125642240 | bytes 60444856 | solution.py:57
  209.3 19.6 %dynamic_update_slice.51 = f32[2,512,8,64]{1,0,3,2:T(2,128)} dynamic-update-slice(f32[2,512,8,64]{1,0,3,2:T(2,128)} %get-tuple-element.948, f32[1,512,8,64]{1,0,3,2:T(1,128)S(1)} %copy.130, s32[]{:T(128)} %get-tuple-element.947, s32[]{:T(128)} %constant.141.clone.1..sunk.1, s32[]{:T(128)} %constant.141.clone.1..sunk.1, s32[]{:T(128)} %constant.141.clone.1..sunk.1) | dynamic-update-slice | bytes 2097156 | tf_op jit(solution)/shard_map/while/body/jit(dynamic_update_index_in_dim)/dynamic_update_slice | solution.py:57
  246.6 19.6 %dynamic_update_slice.51 = f32[2,512,8,64]{1,0,3,2:T(2,128)} dynamic-update-slice(f32[2,512,8,64]{1,0,3,2:T(2,128)} %get-tuple-element.948, f32[1,512,8,64]{1,0,3,2:T(1,128)S(1)} %copy.130, s32[]{:T(128)} %get-tuple-element.947, s32[]{:T(128)} %constant.141.clone.1..sunk.1, s32[]{:T(128)} %constant.141.clone.1..sunk.1, s32[]{:T(128)} %constant.141.clone.1..sunk.1) | dynamic-update-slice | bytes 2097156 | tf_op jit(solution)/shard_map/while/body/jit(dynamic_update_index_in_dim)/dynamic_update_slice | solution.py:57
  286.0 192.8 %all-reduce.10.cloned.1.call-done = (f32[1024,1024]{1,0:T(8,128)}, f32[1024,1024]{1,0:T(8,128)}) async-done(((f32[1024,1024]{1,0:T(8,128)}, f32[1024,1024]{1,0:T(8,128)}), (f32[1024,1024]{1,0:T(8,128)}, f32[1024,1024]{1,0:T(8,128)})) %all-reduce.10.cloned.1.call-update) | async-done | bytes 8388624 | tf_op jit(solution)/shard_map/psum | solution.py:167
  491.7 22.0 %all-gather.37.cloned.1.call-done = bf16[1,1024,1024]{2,1,0:T(8,128)(2,1)} async-done(((bf16[1,512,1024]{2,1,0:T(8,128)(2,1)}), bf16[1,1024,1024]{2,1,0:T(8,128)(2,1)}) %all-gather.37.cloned.1.call-update) | async-done | bytes 2097168 | tf_op jit(solution)/shard_map/all_gather | solution.py:193
  513.7 52.8 %all-gather.25.cloned.1.call-done = bf16[2048,1024]{0,1:T(8,128)(2,1)} async-done(((bf16[2048,64]{0,1:T(8,128)(2,1)}), bf16[2048,1024]{0,1:T(8,128)(2,1)}) %all-gather.25.cloned.1.call-update) | async-done | bytes 4194320 | tf_op jit(solution)/shard_map/all_gather | solution.py:128
  566.5 10.5 fusion.98
  577.0 40.7 %all-gather.23.cloned.1.call-done = bf16[1024,2048]{1,0:T(8,128)(2,1)} async-done(((bf16[64,2048]{1,0:T(8,128)(2,1)}), bf16[1024,2048]{1,0:T(8,128)(2,1)}) %all-gather.23.cloned.1.call-update) | async-done | bytes 4194320 | tf_op jit(solution)/shard_map/all_gather | solution.py:127
  617.7 33.8 %all-gather.21.cloned.1.call-done = bf16[1024,1024]{1,0:T(8,128)(2,1)} async-done(((bf16[512,1024]{1,0:T(8,128)(2,1)}), bf16[1024,1024]{1,0:T(8,128)(2,1)}) %all-gather.21.cloned.1.call-update) | async-done | bytes 2097168 | tf_op jit(solution)/shard_map/all_gather | solution.py:175
  651.5 10.2 fusion.120
  661.7 24.3 %all-gather.29.cloned.1.call-done = bf16[1024,1024]{1,0:T(8,128)(2,1)} async-done(((bf16[512,1024]{1,0:T(8,128)(2,1)}), bf16[1024,1024]{1,0:T(8,128)(2,1)}) %all-gather.29.cloned.1.call-update) | async-done | bytes 2097168 | tf_op jit(solution)/shard_map/all_gather | solution.py:175
  686.0 10.0 fusion.121
  696.0 7.2 all-reduce.3
  703.3 17.8 %all-gather.35.cloned.1.call-done = bf16[1,1024,1024]{2,1,0:T(8,128)(2,1)} async-done(((bf16[1,512,1024]{2,1,0:T(8,128)(2,1)}), bf16[1,1024,1024]{2,1,0:T(8,128)(2,1)}) %all-gather.35.cloned.1.call-update) | async-done | bytes 2097168 | tf_op jit(solution)/shard_map/all_gather | solution.py:193
  721.1 20.2 %multiply_reduce_fusion.3 = (f32[2048]{0:T(1024)}, f32[1024]{0:T(1024)S(1)}, f32[1024]{0:T(1024)S(1)}, f32[1024]{0:T(1024)S(1)}, f32[1024]{0:T(1024)S(1)}, /*index=5*/f32[2048]{0:T(1024)}, f32[1024,2048]{1,0:T(8,128)}) fusion(f32[1024]{0:T(1024)S(1)} %get-tuple-element.645, f32[1024]{0:T(1024)S(1)} %get-tuple-element.644, ...), kind=kOutput, calls=%fused_computation.90 | convolution fusion | flops 4362067968 | bytes 39903232 | tf_op jit(solution)/shard_map/gd,fd->gf/dot_general | solution.py:197
  741.3 6.9 all-reduce.2
  748.2 22.7 %fusion.54 = (bf16[1024,2048]{1,0:T(8,128)(2,1)S(1)}, bf16[1024,2048]{1,0:T(8,128)(2,1)}, bf16[1024,2048]{1,0:T(8,128)(2,1)}) fusion(f32[1024,2048]{1,0:T(8,128)} %get-tuple-element.655, f32[1024,2048]{1,0:T(8,128)} %get-tuple-element.656, f32[1024]{0:T(1024)S(1)} %get-tuple-element.592, f32[1024]{0:T(1024)S(1)} %broadcast_multiply_fusion.1, ...), kind=kLoop, calls=%fused_computation.80 | loop fusion | flops 125829120 | bytes 46178304 | tf_op jit(solution)/shard_map/convert_element_type | solution.py:211
  779.0 9.3 convolution_convert_fusion.1
  788.4 9.9 fusion.131
  798.4 11.1 convolution_convert_fusion
  809.6 25.0 %reduce-scatter.14.cloned.1.call-done = f32[512,1024]{1,0:T(8,128)} async-done(((f32[1024,1024]{1,0:T(8,128)}), f32[512,1024]{1,0:T(8,128)}) %reduce-scatter.14.cloned.1.call-update) | async-done | bytes 2097168 | tf_op jit(solution)/shard_map/reduce_scatter | solution.py:215
  837.6 31.8 %reduce-scatter.10.cloned.1.call-done = bf16[512,1024]{1,0:T(8,128)(2,1)} async-done(((bf16[1024,1024]{1,0:T(8,128)(2,1)}), bf16[512,1024]{1,0:T(8,128)(2,1)}) %reduce-scatter.10.cloned.1.call-update) | async-done | bytes 1048592 | tf_op jit(solution)/shard_map/reduce_scatter | solution.py:185
  869.3 56.5 %reduce-scatter.18.cloned.1.call-done = f32[512,1024]{1,0:T(8,128)} async-done(((f32[1024,1024]{1,0:T(8,128)}), f32[512,1024]{1,0:T(8,128)}) %reduce-scatter.18.cloned.1.call-update) | async-done | bytes 2097168 | tf_op jit(solution)/shard_map/reduce_scatter | solution.py:215
  925.8 7.2 multiply_reduce_fusion.15
  933.1 26.8 %reduce-scatter.12.cloned.1.call-done = bf16[512,1024]{1,0:T(8,128)(2,1)} async-done(((bf16[1024,1024]{1,0:T(8,128)(2,1)}), bf16[512,1024]{1,0:T(8,128)(2,1)}) %reduce-scatter.12.cloned.1.call-update) | async-done | bytes 1048592 | tf_op jit(solution)/shard_map/reduce_scatter | solution.py:185
  969.2 7.6 fusion.100
  976.8 10.9 add_convert_fusion
  989.2 6.5 fusion.132
  1008.6 27.7 %all-gather.31.cloned.1.call-done = bf16[1024,1024]{1,0:T(8,128)(2,1)} async-done(((bf16[512,1024]{1,0:T(8,128)(2,1)}), bf16[1024,1024]{1,0:T(8,128)(2,1)}) %all-gather.31.cloned.1.call-update) | async-done | bytes 2097168 | tf_op jit(solution)/shard_map/all_gather | solution.py:227
  1043.9 123.0 %while.60 = (s32[]{:T(128)}, f32[1024,8,64]{0,2,1:T(8,128)}, f32[1024,8,64]{0,2,1:T(8,128)}, bf16[2,512,8,64]{1,3,2,0:T(8,128)(2,1)}, s32[2]{0:T(128)S(1)}, /*in...) while((s32[]{:T(128)}, f32[1024,8,64]{0,2,1:T(8,128)}, ...), condition=%wide.region_47.48_spmd.clone.clone, body=%wide.region_45.47_spmd.clone.clone.sunk | while | flops 2726555648 | bytes 208769808 | solution.py:104
  1047.5 10.5 fusion.228
  1058.0 13.9 multiply_reduce_fusion.30
  1071.9 14.9 multiply_convert_fusion.20
  1086.9 6.7 bitcast_add_fusion.8
  1093.6 7.6 fusion.229
  1108.5 9.6 fusion.228
  1118.1 13.7 multiply_reduce_fusion.30
  1131.8 15.4 multiply_convert_fusion.20
  1147.2 7.2 bitcast_add_fusion.8
  1154.5 7.6 fusion.229
  1168.0 119.8 %while.61 = (s32[]{:T(128)}, f32[1024,8,64]{0,2,1:T(8,128)}, f32[1024,8,64]{0,2,1:T(8,128)}, bf16[2,512,8,64]{1,3,2,0:T(8,128)(2,1)}, s32[2]{0:T(128)S(1)}, /*in...) while((s32[]{:T(128)}, f32[1024,8,64]{0,2,1:T(8,128)}, ...), condition=%wide.region_62.63_spmd.clone.clone, body=%wide.region_60.62_spmd.clone.clone.sunk | while | flops 2726555648 | bytes 212964144 | solution.py:104
  1171.4 9.6 fusion.239
  1181.0 13.7 multiply_reduce_fusion.31
  1194.7 14.8 multiply_convert_fusion.21
  1209.5 6.7 bitcast_add_fusion.10
  1216.2 7.7 fusion.240
  1230.1 9.6 fusion.239
  1239.7 13.6 multiply_reduce_fusion.31
  1253.3 14.8 multiply_convert_fusion.21
  1268.1 7.3 bitcast_add_fusion.10
  1275.4 7.7 fusion.240
  1311.4 6.2 fusion.106
  1334.3 7.4 bitcast_convert_fusion
  1341.8 7.0 bitcast_convert_fusion.1
  1357.3 81.9 %all-reduce.8.cloned.1.call-done = bf16[3,1024,512]{2,0,1:T(4,128)(2,1)} async-done(((bf16[3,1024,512]{2,0,1:T(4,128)(2,1)}), bf16[3,1024,512]{2,0,1:T(4,128)(2,1)}) %all-reduce.8.cloned.1.call-update) | async-done | bytes 3145744
  1441.1 58.6 %reduce-scatter.22.cloned.1.call-done = bf16[512,64]{0,1:T(8,128)(2,1)} async-done(((bf16[512,1024]{0,1:T(8,128)(2,1)}), bf16[512,64]{0,1:T(8,128)(2,1)}) %reduce-scatter.22.cloned.1.call-update) | async-done | bytes 65552 | tf_op jit(solution)/shard_map/reduce_scatter | solution.py:267
  1501.2 31.6 %reduce-scatter.20.cloned.1.call-done = bf16[512,1024]{1,0:T(8,128)(2,1)} async-done(((bf16[1024,1024]{1,0:T(8,128)(2,1)}), bf16[512,1024]{1,0:T(8,128)(2,1)}) %reduce-scatter.20.cloned.1.call-update) | async-done | bytes 1048592 | tf_op jit(solution)/shard_map/reduce_scatter | solution.py:249
  1532.8 34.8 %reduce-scatter.16.cloned.1.call-done = bf16[512,1024]{1,0:T(8,128)(2,1)} async-done(((bf16[1024,1024]{1,0:T(8,128)(2,1)}), bf16[512,1024]{1,0:T(8,128)(2,1)}) %reduce-scatter.16.cloned.1.call-update) | async-done | bytes 1048592 | tf_op jit(solution)/shard_map/reduce_scatter | solution.py:249
  1570.9 39.8 %all-reduce.1 = (f32[3,1024]{1,0:T(4,128)}, f32[16]{0:T(128)S(1)}, f32[4096]{0:T(1024)S(1)}) all-reduce(f32[3,1024]{1,0:T(4,128)S(1)} %pad_maximum_fusion.8, f32[16]{0:T(128)S(1)} %add_dynamic-update-slice_fusion.1, f32[4096]{0:T(1024)S(1)} %add_dynamic-update-slice_fusion), channel_id=1, replica_groups=mesh['batch'=16,'tensor'=2] {'batch','tensor'}, use_global_device_ids=true, to_apply=%region_72.73 | all-reduce | flops 7184 | bytes 57472 | tf_op jit(solution)/shard_map/psum | solution.py:286
  (405 shorter events, 250.3 us)
Async XLA Ops:
  7.2 41.6 %all-gather.15.cloned.1.call-start = ((), (), s32[]{:S(2)}) async-start(), calls=%async_computation.9 | async-start | bytes 3145728 | tf_op jit(solution)/shard_map/all_gather | solution.py:156
  12.8 83.4 %all-gather.17.cloned.1.call-start = ((), (), s32[]{:S(2)}) async-start(), calls=%async_computation.10 | async-start | bytes 3342336 | tf_op jit(solution)/shard_map/all_gather | solution.py:125
  13.6 167.3 %all-gather.27.cloned.1.call-start = ((), (), s32[]{:S(2)}) async-start(), calls=%async_computation.16 | async-start | bytes 3145728 | tf_op jit(solution)/shard_map/all_gather | solution.py:156
  14.3 258.1 %all-gather.19.cloned.1.call-start = ((), (), s32[]{:S(2)}) async-start(), calls=%async_computation.11 | async-start | bytes 1114112 | tf_op jit(solution)/shard_map/all_gather | solution.py:126
  14.9 463.9 %all-reduce.10.cloned.1.call-start = ((), (), s32[]{:S(2)}) async-start(), calls=%async_computation.31 | async-start | bytes 16777216 | tf_op jit(solution)/shard_map/psum | solution.py:167
  180.9 7.3 copy-start.46
  266.4 6.0 copy-start.2
  266.4 6.0 copy-start.8
  266.4 6.0 copy-start.48
  281.3 232.4 %all-gather.37.cloned.1.call-start = ((), (), s32[]{:S(2)}) async-start(), calls=%async_computation.29 | async-start | bytes 3145728 | tf_op jit(solution)/shard_map/all_gather | solution.py:193
  284.4 282.0 %all-gather.25.cloned.1.call-start = ((), (), s32[]{:S(2)}) async-start(), calls=%async_computation.14 | async-start | bytes 4456448 | tf_op jit(solution)/shard_map/all_gather | solution.py:128
  285.2 332.5 %all-gather.23.cloned.1.call-start = ((), (), s32[]{:S(2)}) async-start(), calls=%async_computation.13 | async-start | bytes 4456448 | tf_op jit(solution)/shard_map/all_gather | solution.py:127
  285.9 365.5 %all-gather.21.cloned.1.call-start = ((), (), s32[]{:S(2)}) async-start(), calls=%async_computation.12 | async-start | bytes 3145728 | tf_op jit(solution)/shard_map/all_gather | solution.py:175
  490.3 195.7 %all-gather.29.cloned.1.call-start = ((), (), s32[]{:S(2)}) async-start(), calls=%async_computation.17 | async-start | bytes 3145728 | tf_op jit(solution)/shard_map/all_gather | solution.py:175
  490.9 230.2 %all-gather.35.cloned.1.call-start = ((), (), s32[]{:S(2)}) async-start(), calls=%async_computation.28 | async-start | bytes 3145728 | tf_op jit(solution)/shard_map/all_gather | solution.py:193
  491.6 342.9 %reduce-scatter.14.cloned.1.call-start = ((), (), s32[]{:S(2)}) async-start(), calls=%async_computation.19 | async-start | bytes 6291456 | tf_op jit(solution)/shard_map/reduce_scatter | solution.py:215
  661.7 59.4 %copy-start.73 = (f32[2048]{0:T(1024)S(1)}, f32[2048]{0:T(1024)}, u32[]{:S(2)}) copy-start(f32[2048]{0:T(1024)} %param.25) | copy-start | bytes 24580
  748.2 24.7 %copy-start.77 = (bf16[1024,2048]{1,0:T(8,128)(2,1)S(1)}, bf16[1024,2048]{1,0:T(8,128)(2,1)}, u32[]{:S(2)}) copy-start(bf16[1024,2048]{1,0:T(8,128)(2,1)} %all-gather.23.cloned.1.call-done) | copy-start | bytes 12582916
  779.0 90.4 %reduce-scatter.10.cloned.1.call-start = ((), (), s32[]{:S(2)}) async-start(), calls=%async_computation.15 | async-start | bytes 3145728 | tf_op jit(solution)/shard_map/reduce_scatter | solution.py:185
  788.4 137.5 %reduce-scatter.18.cloned.1.call-start = ((), (), s32[]{:S(2)}) async-start(), calls=%async_computation.22 | async-start | bytes 6291456 | tf_op jit(solution)/shard_map/reduce_scatter | solution.py:215
  798.3 161.5 %reduce-scatter.12.cloned.1.call-start = ((), (), s32[]{:S(2)}) async-start(), calls=%async_computation.18 | async-start | bytes 3145728 | tf_op jit(solution)/shard_map/reduce_scatter | solution.py:185
  809.5 192.5 %all-gather.33.cloned.1.call-start = ((), (), s32[]{:S(2)}) async-start(), calls=%async_computation.23 | async-start | bytes 3145728 | tf_op jit(solution)/shard_map/all_gather | solution.py:227
  933.1 32.7 %copy-start.23 = (f32[512,1024]{1,0:T(8,128)S(1)}, f32[512,1024]{1,0:T(8,128)}, u32[]{:S(2)}) copy-start(f32[512,1024]{1,0:T(8,128)} %get-tuple-element.600) | copy-start | bytes 6291460
  959.9 6.3 copy-start.22
  968.5 67.8 %all-gather.31.cloned.1.call-start = ((), (), s32[]{:S(2)}) async-start(), calls=%async_computation.20 | async-start | bytes 3145728 | tf_op jit(solution)/shard_map/all_gather | solution.py:227
  969.1 7.6 copy-start.79
  969.1 381.1 %reduce-scatter.26.cloned.1.call-start = ((), (), s32[]{:S(2)}) async-start(), calls=%async_computation.27 | async-start | bytes 4456448 | tf_op jit(solution)/shard_map/reduce_scatter | solution.py:273
  987.6 364.4 %reduce-scatter.24.cloned.1.call-start = ((), (), s32[]{:S(2)}) async-start(), calls=%async_computation.26 | async-start | bytes 4456448 | tf_op jit(solution)/shard_map/reduce_scatter | solution.py:270
  989.2 6.6 copy-start.33
  989.2 6.6 copy-start.81
  1002.0 437.3 %all-reduce.8.cloned.1.call-start = ((), (), s32[]{:S(2)}) async-start(), calls=%async_computation.30 | async-start | bytes 8388608
  1008.6 32.1 %copy-start.75 = (f32[8]{0:T(128)S(1)}, f32[8]{0:T(128)}, u32[]{:S(2)}) copy-start(f32[8]{0:T(128)} %param.22) | copy-start | bytes 100
  1043.9 124.1 %copy-start.3 = (bf16[1024,8,64]{0,2,1:T(8,128)(2,1)S(1)}, bf16[1024,8,64]{0,2,1:T(8,128)(2,1)}, u32[]{:S(2)}) copy-start(bf16[1024,8,64]{0,2,1:T(8,128)(2,1)} %copy-done.2) | copy-start | bytes 3145732
  1043.9 124.1 %copy-start.37 = (s32[1024]{0:T(1024)S(1)}, s32[1024]{0:T(1024)}, u32[]{:S(2)}) copy-start(s32[1024]{0:T(1024)} %convert_reduce_fusion.2) | copy-start | bytes 12292
  1043.9 124.1 %copy-start.49 = (f32[2,8,512]{2,1,0:T(8,128)S(1)}, f32[2,8,512]{2,1,0:T(8,128)}, u32[]{:S(2)}) copy-start(f32[2,8,512]{2,1,0:T(8,128)} %copy-done.48) | copy-start | bytes 98308
  1086.9 14.3 copy-start
  1147.2 14.9 copy-start
  1209.5 14.4 copy-start.1
  1216.2 7.7 copy-start.16
  1268.1 15.0 copy-start.1
  1275.4 7.7 copy-start.16
  1287.8 7.9 copy-start.7
  1301.2 6.5 copy-start.6
  1311.4 6.3 copy-start.41
  1311.4 6.3 copy-start.44
  1311.4 6.3 copy-start.45
  1311.4 6.3 copy-start.78
  1327.4 172.2 %reduce-scatter.22.cloned.1.call-start = ((), (), s32[]{:S(2)}) async-start(), calls=%async_computation.25 | async-start | bytes 1114112 | tf_op jit(solution)/shard_map/reduce_scatter | solution.py:267
  1334.2 7.6 copy-start.40
  1334.2 7.6 copy-start.43
  1334.2 198.6 %reduce-scatter.20.cloned.1.call-start = ((), (), s32[]{:S(2)}) async-start(), calls=%async_computation.24 | async-start | bytes 3145728 | tf_op jit(solution)/shard_map/reduce_scatter | solution.py:249
  1341.7 7.2 copy-start.82
  1341.7 8.5 copy-start.69
  1341.8 8.5 copy-start.70
  1341.8 225.8 %reduce-scatter.16.cloned.1.call-start = ((), (), s32[]{:S(2)}) async-start(), calls=%async_computation.21 | async-start | bytes 3145728 | tf_op jit(solution)/shard_map/reduce_scatter | solution.py:249
  1348.9 7.9 copy-start.71
  1348.9 8.0 copy-start.72
  1353.8 213.7 %copy-start.12 = (bf16[2,512,1024]{2,1,0:T(8,128)(2,1)S(1)}, bf16[2,512,1024]{2,1,0:T(8,128)(2,1)}, u32[]{:S(2)}) copy-start(bf16[2,512,1024]{2,1,0:T(8,128)(2,1)} %param.18) | copy-start | bytes 6291460
  1353.8 213.7 %copy-start.53 = (f32[1,1024]{1,0:T(1,128)S(1)}, f32[1,1024]{1,0:T(1,128)}, u32[]{:S(2)}) copy-start(f32[1,1024]{1,0:T(1,128)} %copy-done.52) | copy-start | bytes 12292
  1353.8 213.7 %copy-start.55 = (f32[512]{0:T(512)S(1)}, f32[512]{0:T(512)}, u32[]{:S(2)}) copy-start(f32[512]{0:T(512)} %copy-done.54) | copy-start | bytes 6148
  1353.8 213.7 %copy-start.57 = (f32[512]{0:T(512)S(1)}, f32[512]{0:T(512)}, u32[]{:S(2)}) copy-start(f32[512]{0:T(512)} %copy-done.56) | copy-start | bytes 6148
  1353.8 213.7 %copy-start.61 = (f32[512]{0:T(512)S(1)}, f32[512]{0:T(512)}, u32[]{:S(2)}) copy-start(f32[512]{0:T(512)} %copy-done.60) | copy-start | bytes 6148
  1353.9 213.7 %copy-start.63 = (f32[512]{0:T(512)S(1)}, f32[512]{0:T(512)}, u32[]{:S(2)}) copy-start(f32[512]{0:T(512)} %copy-done.62) | copy-start | bytes 6148
  1532.8 79.1 %copy-start.30 = (bf16[512,1024]{1,0:T(8,128)(2,1)S(1)}, bf16[512,1024]{1,0:T(8,128)(2,1)}, u32[]{:S(2)}) copy-start(bf16[512,1024]{1,0:T(8,128)(2,1)} %reduce-scatter.20.cloned.1.call-done) | copy-start | bytes 3145732
  (47 other events, 152.3 us)
Sparse Core Ops, SparseCore 0:
  12.9 35.8 all-gather.14
  51.0 45.2 all-gather.16
  97.8 31.9 all-gather.26
  131.7 37.9 all-gather.18
  281.4 197.3 all-reduce.9
  480.2 33.4 all-gather.36
  515.9 50.5 all-gather.24
  568.6 49.0 all-gather.22
  619.8 31.5 all-gather.20
  652.9 33.1 all-gather.28
  687.6 33.4 all-gather.34
  779.1 55.4 reduce-scatter.13
  837.5 31.8 reduce-scatter.9
  871.5 54.3 reduce-scatter.17
  928.0 31.8 reduce-scatter.11
  968.6 33.1 all-gather.32
  1003.2 33.1 all-gather.30
  1040.1 72.4 reduce-scatter.25
  1116.9 71.3 reduce-scatter.23
  1327.5 111.6 all-reduce.7
  1443.3 56.3 reduce-scatter.21
  1501.9 30.8 reduce-scatter.19
  1535.7 31.8 reduce-scatter.15
where the time goes:
time: 1640 us; the launch traced here: 1620 us
  waiting for transfers between devices  844 us (51%)
  matrix products  385 us (23%)
  other arithmetic  160 us (10%)
  local copies, waits for them, and re-layouts  146 us (9%)
  blocking collectives  53.9 us (3%)
  loops' own time  17.1 us (1%)
    psum x1, waiting for transfers between devices, body(): lax.psum(jnp.dot(scaled, out_full, preferred_element_type=jnp.float32), '...  193 us
    unnamed x24, waiting for transfers between devices  87.2 us
    dynamic_update_slice x8, local copies, waits for them, and re-layouts, attend_forward(): attended, log_sums = lax.map(one_block, firsts)  82.7 us
    reduce_scatter x2, waiting for transfers between devices, body(): lax.psum_scatter(jnp.einsum('gf,df->gd', hidden_grad, up_full, preferred_...  81.5 us
    dot_general x8, matrix products, one_block(): jnp.einsum('qhd,khd->hqk', query_block, all_keys, preferred_element_type=...  73.6 us
    reduce_scatter x2, waiting for transfers between devices, body(): lax.psum_scatter(jnp.einsum('cge,cde->gd', proj_grads, qkv_full, preferre...  66.4 us
    convert_element_type x4, other arithmetic, one_block(): score_grad = (probs * (prob_grad - inner)).astype(jnp.bfloat16)  60 us
    reduce_scatter x2, waiting for transfers between devices, body(): lax.psum_scatter(jnp.dot(narrow, down_full, preferred_element_type=jnp.fl...  58.6 us
  transfers between devices with their start and end apart: 23, of which 18 were waited for; matrix products, arithmetic and copies ran while one was open for 37% of the time, Pallas kernels for 0%

commit v1 on v0

--- a/solution.py
+++ b/solution.py
@@ -164,8 +164,9 @@
             queries, all_keys, values, seg_ids, places, block_rows, factor
         )
         scaled = (attended * head_scale[None, :, None]).astype(jnp.bfloat16).reshape(group_rows, -1)
-        whole_mixed = lax.psum(
-            jnp.dot(scaled, out_full, preferred_element_type=jnp.float32), "tensor"
+        whole_mixed = jnp.sum(
+            lax.all_gather(jnp.dot(scaled, out_full, preferred_element_type=jnp.float32), "tensor"),
+            axis=0,
         )
         mixed_own = lax.dynamic_slice_in_dim(whole_mixed, row_start, own_rows, 0)
         mixed_unit, mixed_factor = normalize(mixed_own)

time: 1640 us -> 1550 us (0.945)
  waiting for transfers between devices: 844 us -> 746 us
    psum x1 -> x0, waiting for transfers between devices: 193 us -> none  [body(): lax.psum(jnp.dot(scaled, out_full, preferred_element_type=jnp.float32), '...]
    all_gather x0 -> x2, waiting for transfers between devices: none -> 103 us  [body(): lax.all_gather(jnp.dot(scaled, out_full, preferred_element_type=jnp.float...]
    unnamed x24 -> x25, waiting for transfers between devices: 87.2 us -> 86.9 us
  transfers between devices with their start and end apart: 23 -> 24, of which waited for: 18 -> 19; matrix products, arithmetic and copies ran while one was open for 37% -> 40% of each run, Pallas kernels for 0% -> 0%
where the time goes in v1:
time: 1550 us; the launch traced here: 1540 us
  waiting for transfers between devices  746 us (48%)
  matrix products  385 us (25%)
  other arithmetic  174 us (11%)
  local copies, waits for them, and re-layouts  149 us (10%)
  blocking collectives  53.9 us (3%)
  loops' own time  16.8 us (1%)
  between operations  16.6 us (1%)
    all_gather x2, waiting for transfers between devices, body(): lax.all_gather(jnp.dot(scaled, out_full, preferred_element_type=jnp.float...  103 us
    unnamed x25, waiting for transfers between devices  86.9 us
    dynamic_update_slice x8, local copies, waits for them, and re-layouts, attend_forward(): attended, log_sums = lax.map(one_block, firsts)  82.7 us
    reduce_scatter x2, waiting for transfers between devices, body(): lax.psum_scatter(jnp.einsum('gf,df->gd', hidden_grad, up_full, preferred_...  81.5 us
    dot_general x8, matrix products, one_block(): jnp.einsum('qhd,khd->hqk', query_block, all_keys, preferred_element_type=...  73.7 us
    reduce_scatter x2, waiting for transfers between devices, body(): lax.psum_scatter(jnp.einsum('cge,cde->gd', proj_grads, qkv_full, preferre...  65.7 us
    convert_element_type x4, other arithmetic, one_block(): score_grad = (probs * (prob_grad - inner)).astype(jnp.bfloat16)  60.1 us
    reduce_scatter x2, waiting for transfers between devices, body(): lax.psum_scatter(jnp.dot(narrow, down_full, preferred_element_type=jnp.fl...  58.6 us
  transfers between devices with their start and end apart: 24, of which 19 were waited for; matrix products, arithmetic and copies ran while one was open for 40% of the time, Pallas kernels for 0%

profile of v1, /device:TPU:0, one launch (start us, length us, event | category | flops | bytes accessed | tf_op | source)
XLA Modules:
  0.0 1542.2 jit_solution(8849034299626364733)
XLA Ops:
  16.8 32.0 %all-gather.19.cloned.1.call-done = bf16[1024,1024]{1,0:T(8,128)(2,1)} async-done(((bf16[512,1024]{1,0:T(8,128)(2,1)}), bf16[1024,1024]{1,0:T(8,128)(2,1)}) %all-gather.19.cloned.1.call-update) | async-done | bytes 2097168 | tf_op jit(solution)/shard_map/all_gather | solution.py:156
  48.8 47.4 %all-gather.21.cloned.1.call-done = bf16[3,1024,512]{2,1,0:T(8,128)(2,1)} async-done(((bf16[3,64,512]{2,1,0:T(8,128)(2,1)}), bf16[3,1024,512]{2,1,0:T(8,128)(2,1)}) %all-gather.21.cloned.1.call-update) | async-done | bytes 3145744 | tf_op jit(solution)/shard_map/all_gather | solution.py:125
  105.5 75.0 %while.58 = (s32[]{:T(128)}, f32[2,512,8,64]{1,0,3,2:T(2,128)}, f32[2,8,512]{2,1,0:T(8,128)S(1)}, s32[2]{0:T(128)S(1)}, s32[1024]{0:T(1024)S(1)}, /*index=5*/s32...) while((s32[]{:T(128)}, f32[2,512,8,64]{1,0,3,2:T(2,128)}, ...), condition=%wide.region_7.8_spmd.clone, body=%wide.region_4.7_spmd.clone.sunk | while | flops 1125642240 | bytes 60444856 | solution.py:57
  123.5 19.6 %dynamic_update_slice.49 = f32[2,512,8,64]{1,0,3,2:T(2,128)} dynamic-update-slice(f32[2,512,8,64]{1,0,3,2:T(2,128)} %get-tuple-element.982, f32[1,512,8,64]{1,0,3,2:T(1,128)S(1)} %copy.131, s32[]{:T(128)} %get-tuple-element.981, s32[]{:T(128)} %constant.141.clone.1..sunk, s32[]{:T(128)} %constant.141.clone.1..sunk, s32[]{:T(128)} %constant.141.clone.1..sunk) | dynamic-update-slice | bytes 2097156 | tf_op jit(solution)/shard_map/while/body/jit(dynamic_update_index_in_dim)/dynamic_update_slice | solution.py:57
  160.9 19.6 %dynamic_update_slice.49 = f32[2,512,8,64]{1,0,3,2:T(2,128)} dynamic-update-slice(f32[2,512,8,64]{1,0,3,2:T(2,128)} %get-tuple-element.982, f32[1,512,8,64]{1,0,3,2:T(1,128)S(1)} %copy.131, s32[]{:T(128)} %get-tuple-element.981, s32[]{:T(128)} %constant.141.clone.1..sunk, s32[]{:T(128)} %constant.141.clone.1..sunk, s32[]{:T(128)} %constant.141.clone.1..sunk) | dynamic-update-slice | bytes 2097156 | tf_op jit(solution)/shard_map/while/body/jit(dynamic_update_index_in_dim)/dynamic_update_slice | solution.py:57
  200.8 75.0 %while.59 = (s32[]{:T(128)}, f32[2,512,8,64]{1,0,3,2:T(2,128)}, f32[2,8,512]{2,1,0:T(8,128)S(1)}, s32[2]{0:T(128)S(1)}, s32[1024]{0:T(1024)S(1)}, /*index=5*/s32...) while((s32[]{:T(128)}, f32[2,512,8,64]{1,0,3,2:T(2,128)}, ...), condition=%wide.region_25.26_spmd.clone, body=%wide.region_22.25_spmd.clone.sunk | while | flops 1125642240 | bytes 60444856 | solution.py:57
  218.7 19.6 %dynamic_update_slice.51 = f32[2,512,8,64]{1,0,3,2:T(2,128)} dynamic-update-slice(f32[2,512,8,64]{1,0,3,2:T(2,128)} %get-tuple-element.946, f32[1,512,8,64]{1,0,3,2:T(1,128)S(1)} %copy.132, s32[]{:T(128)} %get-tuple-element.945, s32[]{:T(128)} %constant.141.clone.1..sunk.1, s32[]{:T(128)} %constant.141.clone.1..sunk.1, s32[]{:T(128)} %constant.141.clone.1..sunk.1) | dynamic-update-slice | bytes 2097156 | tf_op jit(solution)/shard_map/while/body/jit(dynamic_update_index_in_dim)/dynamic_update_slice | solution.py:57
  256.1 19.6 %dynamic_update_slice.51 = f32[2,512,8,64]{1,0,3,2:T(2,128)} dynamic-update-slice(f32[2,512,8,64]{1,0,3,2:T(2,128)} %get-tuple-element.946, f32[1,512,8,64]{1,0,3,2:T(1,128)S(1)} %copy.132, s32[]{:T(128)} %get-tuple-element.945, s32[]{:T(128)} %constant.141.clone.1..sunk.1, s32[]{:T(128)} %constant.141.clone.1..sunk.1, s32[]{:T(128)} %constant.141.clone.1..sunk.1) | dynamic-update-slice | bytes 2097156 | tf_op jit(solution)/shard_map/while/body/jit(dynamic_update_index_in_dim)/dynamic_update_slice | solution.py:57
  292.9 6.7 reduce_sum.467
  299.6 98.8 %all-gather.41.cloned.1.call-done = f32[2048,1024]{1,0:T(8,128)} async-done(((f32[1024,1024]{1,0:T(8,128)}), f32[2048,1024]{1,0:T(8,128)}) %all-gather.41.cloned.1.call-update) | async-done | bytes 8388624 | tf_op jit(solution)/shard_map/all_gather | solution.py:168
  398.4 6.6 reduce_sum.477
  418.4 14.6 all-gather.45.cloned.1.call-done
  433.1 52.8 %all-gather.29.cloned.1.call-done = bf16[2048,1024]{0,1:T(8,128)(2,1)} async-done(((bf16[2048,64]{0,1:T(8,128)(2,1)}), bf16[2048,1024]{0,1:T(8,128)(2,1)}) %all-gather.29.cloned.1.call-update) | async-done | bytes 4194320 | tf_op jit(solution)/shard_map/all_gather | solution.py:128
  485.8 10.5 fusion.98
  496.4 40.9 %all-gather.27.cloned.1.call-done = bf16[1024,2048]{1,0:T(8,128)(2,1)} async-done(((bf16[64,2048]{1,0:T(8,128)(2,1)}), bf16[1024,2048]{1,0:T(8,128)(2,1)}) %all-gather.27.cloned.1.call-update) | async-done | bytes 4194320 | tf_op jit(solution)/shard_map/all_gather | solution.py:127
  537.3 33.6 %all-gather.25.cloned.1.call-done = bf16[1024,1024]{1,0:T(8,128)(2,1)} async-done(((bf16[512,1024]{1,0:T(8,128)(2,1)}), bf16[1024,1024]{1,0:T(8,128)(2,1)}) %all-gather.25.cloned.1.call-update) | async-done | bytes 2097168 | tf_op jit(solution)/shard_map/all_gather | solution.py:176
  570.9 10.2 fusion.120
  581.1 24.5 %all-gather.33.cloned.1.call-done = bf16[1024,1024]{1,0:T(8,128)(2,1)} async-done(((bf16[512,1024]{1,0:T(8,128)(2,1)}), bf16[1024,1024]{1,0:T(8,128)(2,1)}) %all-gather.33.cloned.1.call-update) | async-done | bytes 2097168 | tf_op jit(solution)/shard_map/all_gather | solution.py:176
  605.6 10.0 fusion.121
  615.6 7.2 all-reduce.3
  622.8 17.7 %all-gather.43.cloned.1.call-done = bf16[1,1024,1024]{2,1,0:T(8,128)(2,1)} async-done(((bf16[1,512,1024]{2,1,0:T(8,128)(2,1)}), bf16[1,1024,1024]{2,1,0:T(8,128)(2,1)}) %all-gather.43.cloned.1.call-update) | async-done | bytes 2097168 | tf_op jit(solution)/shard_map/all_gather | solution.py:194
  640.5 20.2 %multiply_reduce_fusion.3 = (f32[2048]{0:T(1024)}, f32[1024]{0:T(1024)S(1)}, f32[1024]{0:T(1024)S(1)}, f32[1024]{0:T(1024)S(1)}, f32[1024]{0:T(1024)S(1)}, /*index=5*/f32[2048]{0:T(1024)}, f32[1024,2048]{1,0:T(8,128)}) fusion(f32[1024]{0:T(1024)S(1)} %get-tuple-element.643, f32[1024]{0:T(1024)S(1)} %get-tuple-element.642, ...), kind=kOutput, calls=%fused_computation.90 | convolution fusion | flops 4362067968 | bytes 39903232 | tf_op jit(solution)/shard_map/gd,fd->gf/dot_general | solution.py:198
  660.6 6.9 all-reduce.2
  667.6 22.7 %fusion.54 = (bf16[1024,2048]{1,0:T(8,128)(2,1)S(1)}, bf16[1024,2048]{1,0:T(8,128)(2,1)}, bf16[1024,2048]{1,0:T(8,128)(2,1)}) fusion(f32[1024,2048]{1,0:T(8,128)} %get-tuple-element.653, f32[1024,2048]{1,0:T(8,128)} %get-tuple-element.654, f32[1024]{0:T(1024)S(1)} %get-tuple-element.592, f32[1024]{0:T(1024)S(1)} %broadcast_multiply_fusion.1, ...), kind=kLoop, calls=%fused_computation.80 | loop fusion | flops 125829120 | bytes 46178304 | tf_op jit(solution)/shard_map/convert_element_type | solution.py:212
  698.4 9.3 convolution_convert_fusion.1
  707.8 9.9 fusion.131
  717.8 11.1 convolution_convert_fusion
  729.0 25.0 %reduce-scatter.14.cloned.1.call-done = f32[512,1024]{1,0:T(8,128)} async-done(((f32[1024,1024]{1,0:T(8,128)}), f32[512,1024]{1,0:T(8,128)}) %reduce-scatter.14.cloned.1.call-update) | async-done | bytes 2097168 | tf_op jit(solution)/shard_map/reduce_scatter | solution.py:216
  757.0 31.6 %reduce-scatter.10.cloned.1.call-done = bf16[512,1024]{1,0:T(8,128)(2,1)} async-done(((bf16[1024,1024]{1,0:T(8,128)(2,1)}), bf16[512,1024]{1,0:T(8,128)(2,1)}) %reduce-scatter.10.cloned.1.call-update) | async-done | bytes 1048592 | tf_op jit(solution)/shard_map/reduce_scatter | solution.py:186
  788.6 56.5 %reduce-scatter.18.cloned.1.call-done = f32[512,1024]{1,0:T(8,128)} async-done(((f32[1024,1024]{1,0:T(8,128)}), f32[512,1024]{1,0:T(8,128)}) %reduce-scatter.18.cloned.1.call-update) | async-done | bytes 2097168 | tf_op jit(solution)/shard_map/reduce_scatter | solution.py:216
  845.1 7.1 multiply_reduce_fusion.15
  852.2 26.9 %reduce-scatter.12.cloned.1.call-done = bf16[512,1024]{1,0:T(8,128)(2,1)} async-done(((bf16[1024,1024]{1,0:T(8,128)(2,1)}), bf16[512,1024]{1,0:T(8,128)(2,1)}) %reduce-scatter.12.cloned.1.call-update) | async-done | bytes 1048592 | tf_op jit(solution)/shard_map/reduce_scatter | solution.py:186
  888.4 7.6 fusion.100
  896.0 10.9 add_convert_fusion
  927.9 27.7 %all-gather.35.cloned.1.call-done = bf16[1024,1024]{1,0:T(8,128)(2,1)} async-done(((bf16[512,1024]{1,0:T(8,128)(2,1)}), bf16[1024,1024]{1,0:T(8,128)(2,1)}) %all-gather.35.cloned.1.call-update) | async-done | bytes 2097168 | tf_op jit(solution)/shard_map/all_gather | solution.py:228
  962.6 123.2 %while.60 = (s32[]{:T(128)}, f32[1024,8,64]{0,2,1:T(8,128)}, f32[1024,8,64]{0,2,1:T(8,128)}, bf16[2,512,8,64]{1,3,2,0:T(8,128)(2,1)}, s32[2]{0:T(128)S(1)}, /*in...) while((s32[]{:T(128)}, f32[1024,8,64]{0,2,1:T(8,128)}, ...), condition=%wide.region_47.48_spmd.clone.clone, body=%wide.region_45.47_spmd.clone.clone.sunk | while | flops 2726555648 | bytes 208769808 | solution.py:104
  966.2 10.5 fusion.228
  976.7 14.0 multiply_reduce_fusion.30
  990.7 14.9 multiply_convert_fusion.20
  1005.6 6.8 bitcast_add_fusion.8
  1012.3 7.7 fusion.229
  1027.3 9.6 fusion.228
  1036.9 13.6 multiply_reduce_fusion.30
  1050.5 15.5 %multiply_convert_fusion.20 = bf16[8,512,1024]{2,1,0:T(8,128)(2,1)} fusion(f32[8,512,1024]{2,1,0:T(8,128)} %get-tuple-element.917, f32[8,512,1024]{2,1,0:T(8,128)} %fusion.228, f32[8,512]{1,0:T(8,128)S(1)} %get-tuple-element.918), kind=kLoop, calls=%fused_computation.28.clone.1 | loop fusion | flops 12582912 | bytes 41959424 | tf_op jit(solution)/shard_map/while/body/eval_jaxpr/convert_element_type | solution.py:88
  1066.0 7.3 bitcast_add_fusion.8
  1073.3 7.6 fusion.229
  1086.8 119.6 %while.61 = (s32[]{:T(128)}, f32[1024,8,64]{0,2,1:T(8,128)}, f32[1024,8,64]{0,2,1:T(8,128)}, bf16[2,512,8,64]{1,3,2,0:T(8,128)(2,1)}, s32[2]{0:T(128)S(1)}, /*in...) while((s32[]{:T(128)}, f32[1024,8,64]{0,2,1:T(8,128)}, ...), condition=%wide.region_62.63_spmd.clone.clone, body=%wide.region_60.62_spmd.clone.clone.sunk | while | flops 2726555648 | bytes 212964144 | solution.py:104
  1090.2 9.6 fusion.239
  1099.8 13.7 multiply_reduce_fusion.31
  1113.5 14.8 multiply_convert_fusion.21
  1128.3 6.7 bitcast_add_fusion.10
  1135.0 7.7 fusion.240
  1148.9 9.6 fusion.239
  1158.5 13.6 multiply_reduce_fusion.31
  1172.1 14.8 multiply_convert_fusion.21
  1186.9 7.2 bitcast_add_fusion.10
  1194.1 7.7 fusion.240
  1253.4 7.5 bitcast_convert_fusion
  1261.0 7.0 bitcast_convert_fusion.1
  1276.5 81.6 %all-reduce.6.cloned.1.call-done = bf16[3,1024,512]{2,0,1:T(4,128)(2,1)} async-done(((bf16[3,1024,512]{2,0,1:T(4,128)(2,1)}), bf16[3,1024,512]{2,0,1:T(4,128)(2,1)}) %all-reduce.6.cloned.1.call-update) | async-done | bytes 3145744
  1359.9 58.6 %reduce-scatter.22.cloned.1.call-done = bf16[512,64]{0,1:T(8,128)(2,1)} async-done(((bf16[512,1024]{0,1:T(8,128)(2,1)}), bf16[512,64]{0,1:T(8,128)(2,1)}) %reduce-scatter.22.cloned.1.call-update) | async-done | bytes 65552 | tf_op jit(solution)/shard_map/reduce_scatter | solution.py:268
  1420.0 31.6 %reduce-scatter.20.cloned.1.call-done = bf16[512,1024]{1,0:T(8,128)(2,1)} async-done(((bf16[1024,1024]{1,0:T(8,128)(2,1)}), bf16[512,1024]{1,0:T(8,128)(2,1)}) %reduce-scatter.20.cloned.1.call-update) | async-done | bytes 1048592 | tf_op jit(solution)/shard_map/reduce_scatter | solution.py:250
  1451.6 34.0 %reduce-scatter.16.cloned.1.call-done = bf16[512,1024]{1,0:T(8,128)(2,1)} async-done(((bf16[1024,1024]{1,0:T(8,128)(2,1)}), bf16[512,1024]{1,0:T(8,128)(2,1)}) %reduce-scatter.16.cloned.1.call-update) | async-done | bytes 1048592 | tf_op jit(solution)/shard_map/reduce_scatter | solution.py:250
  1489.0 39.8 %all-reduce.1 = (f32[3,1024]{1,0:T(4,128)}, f32[16]{0:T(128)S(1)}, f32[4096]{0:T(1024)S(1)}) all-reduce(f32[3,1024]{1,0:T(4,128)S(1)} %pad_maximum_fusion.8, f32[16]{0:T(128)S(1)} %add_dynamic-update-slice_fusion.1, f32[4096]{0:T(1024)S(1)} %add_dynamic-update-slice_fusion), channel_id=1, replica_groups=mesh['batch'=16,'tensor'=2] {'batch','tensor'}, use_global_device_ids=true, to_apply=%region_72.73 | all-reduce | flops 7184 | bytes 57472 | tf_op jit(solution)/shard_map/psum | solution.py:287
  (414 shorter events, 270.7 us)
Async XLA Ops:
  7.2 41.6 %all-gather.19.cloned.1.call-start = ((), (), s32[]{:S(2)}) async-start(), calls=%async_computation.9 | async-start | bytes 3145728 | tf_op jit(solution)/shard_map/all_gather | solution.py:156
  12.8 83.4 %all-gather.21.cloned.1.call-start = ((), (), s32[]{:S(2)}) async-start(), calls=%async_computation.10 | async-start | bytes 3342336 | tf_op jit(solution)/shard_map/all_gather | solution.py:125
  13.6 171.1 %all-gather.23.cloned.1.call-start = ((), (), s32[]{:S(2)}) async-start(), calls=%async_computation.11 | async-start | bytes 1114112 | tf_op jit(solution)/shard_map/all_gather | solution.py:126
  14.3 175.7 %all-gather.31.cloned.1.call-start = ((), (), s32[]{:S(2)}) async-start(), calls=%async_computation.16 | async-start | bytes 3145728 | tf_op jit(solution)/shard_map/all_gather | solution.py:156
  14.9 278.1 %all-gather.39.cloned.1.call-start = ((), (), s32[]{:S(2)}) async-start(), calls=%async_computation.28 | async-start | bytes 12582912 | tf_op jit(solution)/shard_map/all_gather | solution.py:168
  180.5 9.4 copy-start.2
  180.5 9.4 copy-start.8
  180.5 9.4 copy-start.38
  180.5 9.4 copy-start.46
  189.9 208.4 %all-gather.41.cloned.1.call-start = ((), (), s32[]{:S(2)}) async-start(), calls=%async_computation.29 | async-start | bytes 12582912 | tf_op jit(solution)/shard_map/all_gather | solution.py:168
  275.8 7.6 copy-start.4
  275.9 7.6 copy-start.9
  275.9 7.6 copy-start.48
  275.9 7.6 copy-start.85
  283.5 149.6 %all-gather.45.cloned.1.call-start = ((), (), s32[]{:S(2)}) async-start(), calls=%async_computation.31 | async-start | bytes 3145728 | tf_op jit(solution)/shard_map/all_gather | solution.py:194
  286.7 199.1 %all-gather.29.cloned.1.call-start = ((), (), s32[]{:S(2)}) async-start(), calls=%async_computation.14 | async-start | bytes 4456448 | tf_op jit(solution)/shard_map/all_gather | solution.py:128
  287.5 249.8 %all-gather.27.cloned.1.call-start = ((), (), s32[]{:S(2)}) async-start(), calls=%async_computation.13 | async-start | bytes 4456448 | tf_op jit(solution)/shard_map/all_gather | solution.py:127
  288.2 282.6 %all-gather.25.cloned.1.call-start = ((), (), s32[]{:S(2)}) async-start(), calls=%async_computation.12 | async-start | bytes 3145728 | tf_op jit(solution)/shard_map/all_gather | solution.py:176
  417.1 188.5 %all-gather.33.cloned.1.call-start = ((), (), s32[]{:S(2)}) async-start(), calls=%async_computation.17 | async-start | bytes 3145728 | tf_op jit(solution)/shard_map/all_gather | solution.py:176
  417.8 222.7 %all-gather.43.cloned.1.call-start = ((), (), s32[]{:S(2)}) async-start(), calls=%async_computation.30 | async-start | bytes 3145728 | tf_op jit(solution)/shard_map/all_gather | solution.py:194
  418.4 335.6 %reduce-scatter.14.cloned.1.call-start = ((), (), s32[]{:S(2)}) async-start(), calls=%async_computation.19 | async-start | bytes 6291456 | tf_op jit(solution)/shard_map/reduce_scatter | solution.py:216
  581.1 59.4 %copy-start.74 = (f32[2048]{0:T(1024)S(1)}, f32[2048]{0:T(1024)}, u32[]{:S(2)}) copy-start(f32[2048]{0:T(1024)} %param.25) | copy-start | bytes 24580
  667.6 24.7 %copy-start.78 = (bf16[1024,2048]{1,0:T(8,128)(2,1)S(1)}, bf16[1024,2048]{1,0:T(8,128)(2,1)}, u32[]{:S(2)}) copy-start(bf16[1024,2048]{1,0:T(8,128)(2,1)} %all-gather.27.cloned.1.call-done) | copy-start | bytes 12582916
  698.4 90.2 %reduce-scatter.10.cloned.1.call-start = ((), (), s32[]{:S(2)}) async-start(), calls=%async_computation.15 | async-start | bytes 3145728 | tf_op jit(solution)/shard_map/reduce_scatter | solution.py:186
  707.8 137.3 %reduce-scatter.18.cloned.1.call-start = ((), (), s32[]{:S(2)}) async-start(), calls=%async_computation.22 | async-start | bytes 6291456 | tf_op jit(solution)/shard_map/reduce_scatter | solution.py:216
  717.8 161.4 %reduce-scatter.12.cloned.1.call-start = ((), (), s32[]{:S(2)}) async-start(), calls=%async_computation.18 | async-start | bytes 3145728 | tf_op jit(solution)/shard_map/reduce_scatter | solution.py:186
  729.0 192.3 %all-gather.37.cloned.1.call-start = ((), (), s32[]{:S(2)}) async-start(), calls=%async_computation.23 | async-start | bytes 3145728 | tf_op jit(solution)/shard_map/all_gather | solution.py:228
  852.2 32.9 %copy-start.24 = (f32[512,1024]{1,0:T(8,128)S(1)}, f32[512,1024]{1,0:T(8,128)}, u32[]{:S(2)}) copy-start(f32[512,1024]{1,0:T(8,128)} %get-tuple-element.598) | copy-start | bytes 6291460
  887.7 67.8 %all-gather.35.cloned.1.call-start = ((), (), s32[]{:S(2)}) async-start(), calls=%async_computation.20 | async-start | bytes 3145728 | tf_op jit(solution)/shard_map/all_gather | solution.py:228
  888.3 7.6 copy-start.81
  888.3 381.1 %reduce-scatter.26.cloned.1.call-start = ((), (), s32[]{:S(2)}) async-start(), calls=%async_computation.27 | async-start | bytes 4456448 | tf_op jit(solution)/shard_map/reduce_scatter | solution.py:274
  906.9 364.4 %reduce-scatter.24.cloned.1.call-start = ((), (), s32[]{:S(2)}) async-start(), calls=%async_computation.26 | async-start | bytes 4456448 | tf_op jit(solution)/shard_map/reduce_scatter | solution.py:271
  908.4 6.6 copy-start.83
  921.2 34.4 %copy-start.20 = (f32[64,8,2,512]{3,1,2,0:T(8,128)S(1)}, f32[64,8,2,512]{3,1,2,0:T(8,128)}, u32[]{:S(2)}) copy-start(f32[64,8,2,512]{3,1,2,0:T(8,128)} %copy.127) | copy-start | bytes 6291460
  921.2 436.9 %all-reduce.6.cloned.1.call-start = ((), (), s32[]{:S(2)}) async-start(), calls=%async_computation.32 | async-start | bytes 8388608
  927.9 31.4 %copy-start.76 = (f32[8]{0:T(128)S(1)}, f32[8]{0:T(128)}, u32[]{:S(2)}) copy-start(f32[8]{0:T(128)} %param.22) | copy-start | bytes 100
  962.5 124.3 %copy-start.5 = (bf16[1024,8,64]{0,2,1:T(8,128)(2,1)S(1)}, bf16[1024,8,64]{0,2,1:T(8,128)(2,1)}, u32[]{:S(2)}) copy-start(bf16[1024,8,64]{0,2,1:T(8,128)(2,1)} %copy-done.4) | copy-start | bytes 3145732
  962.5 124.3 %copy-start.37 = (s32[1024]{0:T(1024)S(1)}, s32[1024]{0:T(1024)}, u32[]{:S(2)}) copy-start(s32[1024]{0:T(1024)} %convert_reduce_fusion.2) | copy-start | bytes 12292
  962.5 124.3 %copy-start.49 = (f32[2,8,512]{2,1,0:T(8,128)S(1)}, f32[2,8,512]{2,1,0:T(8,128)}, u32[]{:S(2)}) copy-start(f32[2,8,512]{2,1,0:T(8,128)} %copy-done.48) | copy-start | bytes 98308
  1005.6 14.4 copy-start
  1066.0 14.9 copy-start
  1128.3 14.3 copy-start.1
  1135.0 7.7 copy-start.19
  1186.9 14.9 copy-start.1
  1194.1 7.7 copy-start.19
  1206.5 7.9 copy-start.7
  1219.9 6.6 copy-start.6
  1246.2 172.2 %reduce-scatter.22.cloned.1.call-start = ((), (), s32[]{:S(2)}) async-start(), calls=%async_computation.25 | async-start | bytes 1114112 | tf_op jit(solution)/shard_map/reduce_scatter | solution.py:268
  1253.3 7.7 copy-start.40
  1253.4 7.7 copy-start.43
  1253.4 198.3 %reduce-scatter.20.cloned.1.call-start = ((), (), s32[]{:S(2)}) async-start(), calls=%async_computation.24 | async-start | bytes 3145728 | tf_op jit(solution)/shard_map/reduce_scatter | solution.py:250
  1260.9 7.2 copy-start.84
  1260.9 8.4 copy-start.70
  1260.9 8.4 copy-start.71
  1261.0 224.7 %reduce-scatter.16.cloned.1.call-start = ((), (), s32[]{:S(2)}) async-start(), calls=%async_computation.21 | async-start | bytes 3145728 | tf_op jit(solution)/shard_map/reduce_scatter | solution.py:250
  1268.1 7.9 copy-start.72
  1268.1 8.0 copy-start.73
  1273.0 212.7 %copy-start.12 = (bf16[2,512,1024]{2,1,0:T(8,128)(2,1)S(1)}, bf16[2,512,1024]{2,1,0:T(8,128)(2,1)}, u32[]{:S(2)}) copy-start(bf16[2,512,1024]{2,1,0:T(8,128)(2,1)} %param.18) | copy-start | bytes 6291460
  1273.0 212.7 %copy-start.53 = (f32[1,1024]{1,0:T(1,128)S(1)}, f32[1,1024]{1,0:T(1,128)}, u32[]{:S(2)}) copy-start(f32[1,1024]{1,0:T(1,128)} %copy-done.52) | copy-start | bytes 12292
  1273.0 212.7 %copy-start.55 = (f32[512]{0:T(512)S(1)}, f32[512]{0:T(512)}, u32[]{:S(2)}) copy-start(f32[512]{0:T(512)} %copy-done.54) | copy-start | bytes 6148
  1273.0 212.7 %copy-start.57 = (f32[512]{0:T(512)S(1)}, f32[512]{0:T(512)}, u32[]{:S(2)}) copy-start(f32[512]{0:T(512)} %copy-done.56) | copy-start | bytes 6148
  1273.0 212.7 %copy-start.62 = (f32[512]{0:T(512)S(1)}, f32[512]{0:T(512)}, u32[]{:S(2)}) copy-start(f32[512]{0:T(512)} %copy-done.61) | copy-start | bytes 6148
  1273.0 212.7 %copy-start.64 = (f32[512]{0:T(512)S(1)}, f32[512]{0:T(512)}, u32[]{:S(2)}) copy-start(f32[512]{0:T(512)} %copy-done.63) | copy-start | bytes 6148
  1451.6 78.4 %copy-start.30 = (bf16[512,1024]{1,0:T(8,128)(2,1)S(1)}, bf16[512,1024]{1,0:T(8,128)(2,1)}, u32[]{:S(2)}) copy-start(bf16[512,1024]{1,0:T(8,128)(2,1)} %reduce-scatter.20.cloned.1.call-done) | copy-start | bytes 3145732
  (50 other events, 178.8 us)
Sparse Core Ops, SparseCore 0:
  12.9 35.8 all-gather.18
  51.0 45.2 all-gather.20
  98.4 36.8 all-gather.22
  136.6 32.0 all-gather.30
  190.1 102.8 all-gather.38
  294.3 103.9 all-gather.40
  399.9 33.1 all-gather.44
  435.2 50.5 all-gather.28
  488.0 49.2 all-gather.26
  539.2 31.5 all-gather.24
  572.4 33.1 all-gather.32
  607.0 33.4 all-gather.42
  698.5 55.4 reduce-scatter.13
  756.7 31.8 reduce-scatter.9
  790.7 54.3 reduce-scatter.17
  847.3 31.8 reduce-scatter.11
  887.9 33.1 all-gather.36
  922.4 33.1 all-gather.34
  959.4 72.4 reduce-scatter.25
  1036.1 71.3 reduce-scatter.23
  1246.4 111.6 all-reduce.5
  1362.1 56.3 reduce-scatter.21
  1420.7 30.8 reduce-scatter.19
  1453.8 31.8 reduce-scatter.15
